TPU v7x, 32 devices: a whole 2x2x4 slice. The times are simulated.
32 devices in a mesh: fsdp: 8 (over y, x, core), seq: 4 (over z).
Axes of the slice: x: 2, y: 2, z: 4, core: 2. Of those that a mesh axis runs over, the one named last changes fastest.
Arguments:
- tokens: bfloat16 [16, 2048, 768], P('fsdp', 'seq'), may hold values from -6 to 6
- teacher: bfloat16 [16, 2048, 768], P('fsdp', 'seq'), may hold values from -6 to 6
- segment_ids: int32 [16, 2048], P('fsdp', 'seq'), may hold values from 0 to 3, as said below
- latent_flags: int32 [16, 2048], P('fsdp', 'seq'), may hold values from 0 to 1, as said below
- valid_mask: int32 [16, 2048], P('fsdp', 'seq'), may hold values from 0 to 1, as said below
- attngain: bfloat16 [768], P('fsdp'), may hold values from 0.5 to 1.5
- attnshift: bfloat16 [768], P('fsdp'), may hold values from -4 to 4
- qkvweight: bfloat16 [768, 2304], P('fsdp'), may hold values from -0.3125 to 0.3125
- qvbias: bfloat16 [1536], P('fsdp'), may hold values from -4 to 4
- outweight: bfloat16 [768, 768], P('fsdp'), may hold values from -0.875 to 0.875
- outbias: bfloat16 [768], P('fsdp'), may hold values from -4 to 4
- mlpgain: bfloat16 [768], P('fsdp'), may hold values from 0.5 to 1.5
- mlpshift: bfloat16 [768], P('fsdp'), may hold values from -4 to 4
- fcweight: bfloat16 [768, 3072], P('fsdp'), may hold values from -0.21875 to 0.21875
- fcbias: bfloat16 [3072], P('fsdp'), may hold values from -6 to 6
- projweight: bfloat16 [3072, 768], P('fsdp'), may hold values from -0.109375 to 0.109375
- projbias: bfloat16 [768], P('fsdp'), may hold values from -4 to 4
Outputs:
- distill_loss: float32 [], replicated
- layer_out: bfloat16 [16, 2048, 768], P('fsdp', 'seq')
- grad_tokens: bfloat16 [16, 2048, 768], P('fsdp', 'seq')
- grad_attngain: float32 [768], P('fsdp')
- grad_attnshift: float32 [768], P('fsdp')
- grad_qkvweight: float32 [768, 2304], P('fsdp')
- grad_qvbias: float32 [1536], P('fsdp')
- grad_outweight: float32 [768, 768], P('fsdp')
- grad_outbias: float32 [768], P('fsdp')
- grad_mlpgain: float32 [768], P('fsdp')
- grad_mlpshift: float32 [768], P('fsdp')
- grad_fcweight: float32 [768, 3072], P('fsdp')
- grad_fcbias: float32 [3072], P('fsdp')
- grad_projweight: float32 [3072, 768], P('fsdp')
- grad_projbias: float32 [768], P('fsdp')
Inputs may be any that keep to these rules, and one draw needn't show every extreme that they name: `segment_ids`: ids never fall along a sequence, start at 0, and every sequence holds four documents. `latent_flags`: the first token of every sequence is not latent. `valid_mask`: the first token of every sequence is valid.
All inputs are finite; a program needn't handle non-finite values.
Results may differ from a plain program's by a relative error of at most 0.012.
The roundings to bfloat16 on the way count: a program that leaves them out, or rounds other values in their place, can miss the bound.
Values may be sent and summed in bfloat16 or wider, within the bound.
No kernel may reach another device: no remote copies, remote signals or barrier semaphores. Data moves between devices by JAX's collectives and lax.ppermute only.
A program may use at most 256 MiB of HBM per device.

v0:
```python
import math
import jax
import jax.numpy as jnp
from jax import lax
from jax.sharding import PartitionSpec as P

H = 12
HD = 64
EPSILON = 1e-05


def for_sending(x):

    def short(part):
        return part.astype(jnp.bfloat16) if part.dtype == jnp.float32 else part

    return jax.tree.map(short, x)


def layer_norm(values, gain, shift):
    center = values - jnp.mean(values, -1, keepdims=True)
    spread = jnp.mean(center * center, -1, keepdims=True)
    return center * lax.rsqrt(spread + EPSILON) * gain + shift


def gelu_tanh(values):
    inner = 0.7978845608028654 * (values + 0.044715 * values * values * values)
    return 0.5 * values * (1.0 + jnp.tanh(inner))


def split_heads(joint_item):
    length = joint_item.shape[0]
    heads_local = joint_item.shape[-1] // HD
    query = joint_item[:, 0, 0].reshape(length, heads_local, HD)
    keys = joint_item[:, 1, 0].reshape(length, heads_local, HD)
    values = joint_item[:, 2, 0].reshape(length, heads_local, HD)
    return (query, keys, values)


def block_scores(query_block, keys, segments, start):
    block = query_block.shape[0]
    length = keys.shape[0]
    scale = 1.0 / math.sqrt(HD)
    scores = (
        jnp.einsum("qhd,khd->hqk", query_block, keys, preferred_element_type=jnp.float32) * scale
    )
    place = jnp.arange(length, dtype=jnp.int32)
    rows_here = place[start : start + block]
    allowed = (place[None, :] <= rows_here[:, None]) & (
        segments[start : start + block, None] == segments[None, :]
    )
    return jnp.where(allowed[None], scores, -1e30)


def attend_sequence(item):
    joint_item, segments = item
    query, keys, values = split_heads(joint_item)
    length = query.shape[0]
    block = min(512, length)
    mixed_blocks = []
    total_blocks = []
    for start in range(0, length, block):
        masked = block_scores(query[start : start + block], keys, segments, start)
        highest = jnp.max(masked, -1, keepdims=True)
        powers = jnp.exp(masked - highest)
        total = jnp.sum(powers, -1, keepdims=True)
        probs = powers / total
        mixed = jnp.einsum(
            "hqk,khd->qhd", probs.astype(jnp.bfloat16), values, preferred_element_type=jnp.float32
        )
        mixed_blocks.append(mixed.reshape(block, -1).astype(jnp.bfloat16))
        total_blocks.append((highest + jnp.log(total))[:, :, 0])
    return (jnp.concatenate(mixed_blocks, 0), jnp.concatenate(total_blocks, 1))


def attend_items(pieces):
    joint_piece, segment_piece = pieces
    segments = segment_piece[:, :, 0, 0, 0]
    mixed, log_total = lax.map(attend_sequence, (joint_piece, segments))
    return (mixed, log_total, joint_piece, segments)


def back_sequence(item):
    joint_item, segments, log_total, grad_mixed = item
    query, keys, values = split_heads(joint_item)
    length, heads_local, _ = query.shape
    grad_out = grad_mixed[:, 0].reshape(length, heads_local, HD)
    block = min(512, length)
    scale = 1.0 / math.sqrt(HD)
    grad_keys = jnp.zeros((length, heads_local, HD), jnp.float32)
    grad_values = jnp.zeros((length, heads_local, HD), jnp.float32)
    query_grads = []
    for start in range(0, length, block):
        query_block = query[start : start + block]
        grad_block = grad_out[start : start + block]
        masked = block_scores(query_block, keys, segments, start)
        probs = jnp.exp(masked - log_total[:, start : start + block, None])
        probs_low = probs.astype(jnp.bfloat16)
        grad_values = grad_values + jnp.einsum(
            "hqk,qhd->khd", probs_low, grad_block, preferred_element_type=jnp.float32
        )
        grad_probs = jnp.einsum(
            "qhd,khd->hqk", grad_block, values, preferred_element_type=jnp.float32
        )
        center = jnp.sum(probs * grad_probs, -1, keepdims=True)
        grad_scores = (probs * (grad_probs - center)).astype(jnp.bfloat16)
        query_grads.append(
            jnp.einsum("hqk,khd->qhd", grad_scores, keys, preferred_element_type=jnp.float32)
            * scale
        )
        grad_keys = (
            grad_keys
            + jnp.einsum(
                "hqk,qhd->khd", grad_scores, query_block, preferred_element_type=jnp.float32
            )
            * scale
        )
    grad_query = jnp.concatenate(query_grads, 0)
    stacked = jnp.stack([grad_query, grad_keys, grad_values], 1).astype(jnp.bfloat16)
    return stacked.reshape(length, 3, 1, heads_local * HD)


def local(
    tokens,
    teacher,
    segment_ids,
    latent_flags,
    valid_mask,
    attngain,
    attnshift,
    qkvweight,
    qvbias,
    outweight,
    outbias,
    mlpgain,
    mlpshift,
    fcweight,
    fcbias,
    projweight,
    projbias,
):
    seqs_local, block_len, width = tokens.shape
    groups = lax.axis_size("seq")
    heads_local = H // groups
    rows = seqs_local * block_len
    weight = (valid_mask * (1 - latent_flags)).astype(jnp.float32).reshape(rows)
    local_count = jnp.sum(weight)
    gathered = (
        lax.all_gather(attngain, "fsdp", axis=0, tiled=True),
        lax.all_gather(attnshift, "fsdp", axis=0, tiled=True),
        lax.all_gather(qkvweight, "fsdp", axis=0, tiled=True),
        lax.all_gather(qvbias, "fsdp", axis=0, tiled=True),
        lax.all_gather(outweight, "fsdp", axis=0, tiled=True),
        lax.all_gather(outbias, "fsdp", axis=0, tiled=True),
        lax.all_gather(mlpgain, "fsdp", axis=0, tiled=True),
        lax.all_gather(mlpshift, "fsdp", axis=0, tiled=True),
        lax.all_gather(fcweight, "fsdp", axis=0, tiled=True),
        lax.all_gather(fcbias, "fsdp", axis=0, tiled=True),
        lax.all_gather(projweight, "fsdp", axis=0, tiled=True),
        lax.all_gather(projbias, "fsdp", axis=0, tiled=True),
    )
    first_gain = gathered[0].astype(jnp.float32)
    first_shift = gathered[1].astype(jnp.float32)
    joint_weight = gathered[2]
    joint_bias = gathered[3].astype(jnp.float32)
    merge_weight = gathered[4]
    merge_bias = gathered[5].astype(jnp.float32)
    second_gain = gathered[6].astype(jnp.float32)
    second_shift = gathered[7].astype(jnp.float32)
    up_weight = gathered[8]
    up_bias = gathered[9].astype(jnp.float32)
    down_weight = gathered[10]
    down_bias = gathered[11].astype(jnp.float32)
    inputs = tokens.astype(jnp.float32).reshape(rows, width)
    normed, first_back = jax.vjp(layer_norm, inputs, first_gain, first_shift)
    normed_low = normed.astype(jnp.bfloat16)
    bias_full = jnp.concatenate(
        [joint_bias[:width], jnp.zeros((width,), jnp.float32), joint_bias[width:]]
    )
    joint = jnp.dot(normed_low, joint_weight, preferred_element_type=jnp.float32) + bias_full
    joint_low = joint.astype(jnp.bfloat16).reshape(
        seqs_local, block_len, 3, groups, heads_local * HD
    )
    segment_low = jnp.broadcast_to(
        segment_ids.astype(jnp.bfloat16)[:, :, None, None, None],
        (seqs_local, block_len, 1, groups, 1),
    )
    mixed, log_total, kept_joint, kept_segment = attend_items(
        (
            lax.all_to_all(joint_low, "seq", split_axis=3, concat_axis=1, tiled=True),
            lax.all_to_all(segment_low, "seq", split_axis=3, concat_axis=1, tiled=True),
        )
    )
    length = mixed.shape[1]
    mixed_back = lax.all_to_all(
        for_sending(mixed.reshape(seqs_local, length, 1, heads_local * HD)),
        "seq",
        split_axis=1,
        concat_axis=2,
        tiled=True,
    )
    attended = mixed_back.reshape(rows, width)
    branch = jnp.dot(attended, merge_weight, preferred_element_type=jnp.float32) + merge_bias
    resid = inputs + branch
    normed_two, second_back = jax.vjp(layer_norm, resid, second_gain, second_shift)
    normed_two_low = normed_two.astype(jnp.bfloat16)
    hidden = jnp.dot(normed_two_low, up_weight, preferred_element_type=jnp.float32) + up_bias
    active, gelu_back = jax.vjp(gelu_tanh, hidden)
    active_low = active.astype(jnp.bfloat16)
    result = (
        resid + jnp.dot(active_low, down_weight, preferred_element_type=jnp.float32) + down_bias
    )
    layer_out = result.astype(jnp.bfloat16).reshape(tokens.shape)
    error = result - teacher.astype(jnp.float32).reshape(rows, width)
    local_sum = jnp.sum(weight * jnp.sum(error * error, -1))
    total_sum, total_count = lax.psum((local_sum, local_count), ("fsdp", "seq"))
    distill_loss = total_sum / (width * total_count)
    token_total = rows * lax.axis_size("fsdp") * groups
    factor = token_total / total_count
    grad_result = error * (weight * factor)[:, None]
    back_params = (
        lax.all_gather(attngain, "fsdp", axis=0, tiled=True),
        lax.all_gather(attnshift, "fsdp", axis=0, tiled=True),
        lax.all_gather(qkvweight, "fsdp", axis=0, tiled=True),
        lax.all_gather(qvbias, "fsdp", axis=0, tiled=True),
        lax.all_gather(outweight, "fsdp", axis=0, tiled=True),
        lax.all_gather(outbias, "fsdp", axis=0, tiled=True),
        lax.all_gather(mlpgain, "fsdp", axis=0, tiled=True),
        lax.all_gather(mlpshift, "fsdp", axis=0, tiled=True),
        lax.all_gather(fcweight, "fsdp", axis=0, tiled=True),
        lax.all_gather(fcbias, "fsdp", axis=0, tiled=True),
        lax.all_gather(projweight, "fsdp", axis=0, tiled=True),
        lax.all_gather(projbias, "fsdp", axis=0, tiled=True),
    )
    joint_weight = back_params[2]
    merge_weight = back_params[4]
    up_weight = back_params[8]
    down_weight = back_params[10]
    grad_mlp = grad_result.astype(jnp.bfloat16)
    grad_downbias = jnp.sum(grad_mlp, 0, dtype=jnp.float32)
    grad_downweight = jnp.einsum(
        "rf,rd->fd", active_low, grad_mlp, preferred_element_type=jnp.float32
    )
    grad_active = jnp.einsum("rd,fd->rf", grad_mlp, down_weight, preferred_element_type=jnp.float32)
    grad_hidden = gelu_back(grad_active)[0].astype(jnp.bfloat16)
    grad_upbias = jnp.sum(grad_hidden, 0, dtype=jnp.float32)
    grad_upweight = jnp.einsum(
        "rd,rf->df", normed_two_low, grad_hidden, preferred_element_type=jnp.float32
    )
    grad_normed_two = jnp.einsum(
        "rf,df->rd", grad_hidden, up_weight, preferred_element_type=jnp.float32
    )
    resid_part, grad_secondgain, grad_secondshift = second_back(grad_normed_two)
    grad_resid = grad_result + resid_part
    grad_branch = grad_resid.astype(jnp.bfloat16)
    grad_mergebias = jnp.sum(grad_branch, 0, dtype=jnp.float32)
    grad_mergeweight = jnp.einsum(
        "rd,re->de", attended, grad_branch, preferred_element_type=jnp.float32
    )
    grad_attended = jnp.einsum(
        "re,de->rd", grad_branch, merge_weight, preferred_element_type=jnp.float32
    ).astype(jnp.bfloat16)
    grad_heads = lax.all_to_all(
        grad_attended.reshape(seqs_local, block_len, groups, heads_local * HD),
        "seq",
        split_axis=2,
        concat_axis=1,
        tiled=True,
    )
    grad_joint_heads = lax.map(back_sequence, (kept_joint, kept_segment, log_total, grad_heads))
    grad_joint = lax.all_to_all(
        grad_joint_heads, "seq", split_axis=1, concat_axis=3, tiled=True
    ).reshape(rows, 3 * width)
    grad_jointweight = jnp.einsum(
        "rd,re->de", normed_low, grad_joint, preferred_element_type=jnp.float32
    )
    column_sums = jnp.sum(grad_joint, 0, dtype=jnp.float32)
    grad_jointbias = jnp.concatenate([column_sums[:width], column_sums[2 * width :]])
    grad_normed = jnp.einsum(
        "re,de->rd", grad_joint, joint_weight, preferred_element_type=jnp.float32
    )
    input_part, grad_firstgain, grad_firstshift = first_back(grad_normed)
    grad_tokens = (grad_resid + input_part).astype(jnp.bfloat16).reshape(tokens.shape)
    shards = (
        lax.psum_scatter(grad_firstgain, "fsdp", scatter_dimension=0, tiled=True),
        lax.psum_scatter(grad_firstshift, "fsdp", scatter_dimension=0, tiled=True),
        lax.psum_scatter(grad_jointweight, "fsdp", scatter_dimension=0, tiled=True),
        lax.psum_scatter(grad_jointbias, "fsdp", scatter_dimension=0, tiled=True),
        lax.psum_scatter(grad_mergeweight, "fsdp", scatter_dimension=0, tiled=True),
        lax.psum_scatter(grad_mergebias, "fsdp", scatter_dimension=0, tiled=True),
        lax.psum_scatter(grad_secondgain, "fsdp", scatter_dimension=0, tiled=True),
        lax.psum_scatter(grad_secondshift, "fsdp", scatter_dimension=0, tiled=True),
        lax.psum_scatter(grad_upweight, "fsdp", scatter_dimension=0, tiled=True),
        lax.psum_scatter(grad_upbias, "fsdp", scatter_dimension=0, tiled=True),
        lax.psum_scatter(grad_downweight, "fsdp", scatter_dimension=0, tiled=True),
        lax.psum_scatter(grad_downbias, "fsdp", scatter_dimension=0, tiled=True),
    )
    summed = (
        lax.psum(shards[0].astype(jnp.bfloat16), "seq").astype(jnp.float32),
        lax.psum(shards[1].astype(jnp.bfloat16), "seq").astype(jnp.float32),
        lax.psum(shards[2].astype(jnp.bfloat16), "seq").astype(jnp.float32),
        lax.psum(shards[3].astype(jnp.bfloat16), "seq").astype(jnp.float32),
        lax.psum(shards[4].astype(jnp.bfloat16), "seq").astype(jnp.float32),
        lax.psum(shards[5].astype(jnp.bfloat16), "seq").astype(jnp.float32),
        lax.psum(shards[6].astype(jnp.bfloat16), "seq").astype(jnp.float32),
        lax.psum(shards[7].astype(jnp.bfloat16), "seq").astype(jnp.float32),
        lax.psum(shards[8].astype(jnp.bfloat16), "seq").astype(jnp.float32),
        lax.psum(shards[9].astype(jnp.bfloat16), "seq").astype(jnp.float32),
        lax.psum(shards[10].astype(jnp.bfloat16), "seq").astype(jnp.float32),
        lax.psum(shards[11].astype(jnp.bfloat16), "seq").astype(jnp.float32),
    )
    return (
        distill_loss,
        layer_out,
        grad_tokens,
        summed[0],
        summed[1],
        summed[2],
        summed[3],
        summed[4],
        summed[5],
        summed[6],
        summed[7],
        summed[8],
        summed[9],
        summed[10],
        summed[11],
    )


def solution(mesh):
    placed = (
        P("fsdp", "seq", None),
        P("fsdp", "seq", None),
        P("fsdp", "seq"),
        P("fsdp", "seq"),
        P("fsdp", "seq"),
        P("fsdp"),
        P("fsdp"),
        P("fsdp", None),
        P("fsdp"),
        P("fsdp", None),
        P("fsdp"),
        P("fsdp"),
        P("fsdp"),
        P("fsdp", None),
        P("fsdp"),
        P("fsdp", None),
        P("fsdp"),
    )
    return jax.shard_map(
        local,
        mesh=mesh,
        in_specs=placed,
        out_specs=(
            P(),
            P("fsdp", "seq", None),
            P("fsdp", "seq", None),
            P("fsdp"),
            P("fsdp"),
            P("fsdp", None),
            P("fsdp"),
            P("fsdp", None),
            P("fsdp"),
            P("fsdp"),
            P("fsdp"),
            P("fsdp", None),
            P("fsdp"),
            P("fsdp", None),
            P("fsdp"),
        ),
        check_vma=False,
    )
```

profile of v0, /device:TPU:0, one launch (start us, length us, event | category | flops | bytes accessed | tf_op | source)
XLA Modules:
  0.0 1246.0 jit_solution(2136501249223661194)
XLA Ops:
  19.6 26.6 %all-reduce.17 = (bf16[768]{0:T(1024)(128)(2,1)S(1)}, bf16[768]{0:T(1024)(128)(2,1)S(1)}, bf16[1536]{0:T(1024)(128)(2,1)S(1)}, bf16[768]{0:T(1024)(128)(2,1)}, b...) all-reduce(bf16[768]{0:T(1024)(128)(2,1)S(1)} %dynamic-update-slice, ...), channel_id=1, replica_groups=mesh['fsdp'=8,'seq'=4] {'fsdp'}, use_global_device_ids=true, to_apply=%add.1 | all-reduce | flops 6144 | bytes 24576
  57.7 12.8 %reshape.747 = bf16[2,512,3,4,192]{4,3,2,1,0:T(4,128)(2,1)} reshape(bf16[1024,2304]{1,0:T(8,128)(2,1)} %add_convert_fusion) | data formatting | bytes 9437184 | tf_op jit(solution)/shard_map/reshape | solution.py:181
  70.5 17.3 %copy.86 = bf16[2,512,3,4,192]{1,0,4,2,3:T(2,128)(2,1)} copy(bf16[2,512,3,4,192]{4,3,2,1,0:T(4,128)(2,1)} %reshape.747) | data formatting | bytes 9437184 | tf_op jit(solution)/shard_map/reshape | solution.py:181
  92.9 101.8 %all-to-all-done = bf16[2,512,3,4,192]{1,0,4,2,3:T(2,128)(2,1)} async-done(((bf16[2,512,3,4,192]{1,0,4,2,3:T(2,128)(2,1)}), bf16[2,512,3,4,192]{1,0,4,2,3:T(2,128)(2,1)}, u32[]{:S(2)}, u32[]{:S(2)}) %all-to-all-start) | async-done | bytes 4718624 | tf_op jit(solution)/shard_map/all_to_all | solution.py:190
  216.1 113.0 %while.22 = (s32[]{:T(128)}, bf16[2,2048,192]{1,2,0:T(8,128)(2,1)}, f32[2,3,2048]{2,1,0:T(4,128)S(1)}, bf16[2,2048,3,1,192]{1,4,2,3,0:T(8,128)(2,1)}, bf16[2,204...) while((s32[]{:T(128)}, bf16[2,2048,192]{1,2,0:T(8,128)(2,1)}, ...), condition=%wide.region_11.12_spmd, body=%wide.region_2.11_spmd.sunk | while | flops 3393599488 | bytes 199532768 | solution.py:79
  349.5 38.3 %all-to-all-done.2 = bf16[2,2048,1,192]{3,0,2,1:T(2,128)(2,1)} async-done(((bf16[2,2048,1,192]{3,0,2,1:T(2,128)(2,1)}), bf16[2,2048,1,192]{3,0,2,1:T(2,128)(2,1)}, u32[]{:S(2)}, u32[]{:S(2)}) %all-to-all-start.2) | async-done | bytes 1572896 | tf_op jit(solution)/shard_map/all_to_all | solution.py:195
  387.8 9.3 copy.90
  404.2 11.2 fusion.113
  415.5 13.7 %multiply_reduce_fusion.6 = (f32[1024]{0:T(1024)S(1)}, f32[1024,768]{1,0:T(8,128)}) fusion(bf16[2,512,768]{2,1,0:T(8,128)(2,1)} %param.22, f32[768]{0:T(1024)S(1)} %convert_element_type.248, f32[1024,768]{1,0:T(8,128)S(1)} %copy-done.15, bf16[3072,768]{1,0:T(8,128)(2,1)} %all-gather.12.cloned.1.call-done, f32[1024,3072]{1,0:T(8,128)} %fusion.113, ...), kind=kOutput, calls=%fused_computation.184 | convolution fusion | flops 4868013056 | bytes 25185280 | tf_op jit(solution)/shard_map/dot_general | solution.py:211
  429.8 39.5 %all-reduce.15 = (f32[]{:T(128)}, f32[]{:T(128)}) all-reduce(f32[]{:T(128)} %get-tuple-element.149, f32[]{:T(128)} %get-tuple-element.148), channel_id=1, replica_groups=mesh['fsdp'=8,'seq'=4] {'fsdp','seq'}, use_global_device_ids=true, to_apply=%region_16.17 | all-reduce | flops 2 | bytes 16 | tf_op jit(solution)/shard_map/psum | solution.py:216
  473.6 18.5 %convert_reduce_fusion = (f32[3072]{0:T(1024)}, bf16[1024,3072]{1,0:T(8,128)(2,1)S(1)}) fusion(f32[1024,3072]{1,0:T(8,128)} %fusion.113, f32[3072]{0:T(1024)S(1)} %bitcast.448, bf16[1024,768]{1,0:T(8,128)(2,1)S(1)} %get-tuple-element.202, bf16[3072,768]{1,0:T(8,128)(2,1)} %all-gather.12.cloned.1.call-done), kind=kOutput, calls=%fused_computation.151 | convolution fusion | flops 4916769792 | bytes 25190400 | tf_op jit(solution)/shard_map/rd,fd->rf/dot_general | solution.py:244
  507.8 10.7 fusion.112
  532.8 13.0 %fusion.114 = f32[3072,768]{1,0:T(8,128)} fusion(bf16[1024,768]{1,0:T(8,128)(2,1)S(1)} %copy-done.36, f32[1024,3072]{1,0:T(8,128)} %fusion.113, f32[3072]{0:T(1024)S(1)} %bitcast.449), kind=kOutput, calls=%fused_computation.222 | convolution fusion | flops 4863295488 | bytes 23605248 | tf_op jit(solution)/shard_map/rf,rd->fd/dot_general | solution.py:241
  545.8 23.3 %all-to-all-done.3 = bf16[2,512,4,192]{1,0,3,2:T(2,128)(2,1)S(1)} async-done(((bf16[2,512,4,192]{1,0,3,2:T(2,128)(2,1)}), bf16[2,512,4,192]{1,0,3,2:T(2,128)(2,1)S(1)}, u32[]{:S(2)}, u32[]{:S(2)}) %all-to-all-start.3) | async-done | bytes 1572896 | tf_op jit(solution)/shard_map/all_to_all | solution.py:263
  571.6 315.2 %while.23 = (s32[]{:T(128)}, bf16[2,2048,3,1,192]{1,4,3,2,0:T(8,128)(2,1)}, bf16[2,2048,3,1,192]{1,4,2,3,0:T(8,128)(2,1)}, bf16[2,2048]{1,0:T(2,128)(2,1)S(1)}, ...) while((s32[]{:T(128)}, ...), condition=%wide.region_26.27_spmd, body=%wide.region_21.26_spmd.sunk | while | flops 8274178048 | bytes 657154752 | solution.py:270
  622.7 10.4 multiply_reduce_fusion.14
  633.1 26.1 %multiply_convert_fusion.8 = (bf16[3,512,2048]{2,1,0:T(8,128)(2,1)}, bf16[3,512,2048]{2,1,0:T(8,128)(2,1)}) fusion(f32[3,512,2048]{2,1,0:T(8,128)} %get-tuple-element.454, f32[3,512,2048]{2,1,0:T(8,128)} %copy-done, f32[3,512]{1,0:T(4,128)S(1)} %get-tuple-element.455, f32[3,512]{1,0:T(4,128)S(1)} %get-tuple-element.443, ...), kind=kLoop, calls=%fused_computation.68.clone.1 | loop fusion | flops 37748736 | bytes 65036288 | tf_op jit(solution)/shard_map/while/body/eval_jaxpr/convert_element_type | solution.py:106
  685.9 10.8 multiply_reduce_fusion.15
  696.7 18.2 %multiply_convert_fusion.9 = (bf16[3,512,2048]{2,1,0:T(8,128)(2,1)}, bf16[3,512,2048]{2,1,0:T(8,128)(2,1)}) fusion(f32[3,512,2048]{2,1,0:T(8,128)} %get-tuple-element.460, f32[3,512,2048]{2,1,0:T(8,128)} %fusion.362, f32[3,512]{1,0:T(4,128)} %get-tuple-element.461, f32[3,512]{1,0:T(4,128)S(1)} %get-tuple-element.451, ...), kind=kLoop, calls=%fused_computation.62.clone.1 | loop fusion | flops 37748736 | bytes 65036288 | tf_op jit(solution)/shard_map/while/body/eval_jaxpr/convert_element_type | solution.py:106
  778.6 10.5 multiply_reduce_fusion.14
  789.1 22.8 %multiply_convert_fusion.8 = (bf16[3,512,2048]{2,1,0:T(8,128)(2,1)}, bf16[3,512,2048]{2,1,0:T(8,128)(2,1)}) fusion(f32[3,512,2048]{2,1,0:T(8,128)} %get-tuple-element.454, f32[3,512,2048]{2,1,0:T(8,128)} %copy-done, f32[3,512]{1,0:T(4,128)S(1)} %get-tuple-element.455, f32[3,512]{1,0:T(4,128)S(1)} %get-tuple-element.443, ...), kind=kLoop, calls=%fused_computation.68.clone.1 | loop fusion | flops 37748736 | bytes 65036288 | tf_op jit(solution)/shard_map/while/body/eval_jaxpr/convert_element_type | solution.py:106
  837.1 10.7 multiply_reduce_fusion.15
  847.8 18.1 %multiply_convert_fusion.9 = (bf16[3,512,2048]{2,1,0:T(8,128)(2,1)}, bf16[3,512,2048]{2,1,0:T(8,128)(2,1)}) fusion(f32[3,512,2048]{2,1,0:T(8,128)} %get-tuple-element.460, f32[3,512,2048]{2,1,0:T(8,128)} %fusion.362, f32[3,512]{1,0:T(4,128)} %get-tuple-element.461, f32[3,512]{1,0:T(4,128)S(1)} %get-tuple-element.451, ...), kind=kLoop, calls=%fused_computation.62.clone.1 | loop fusion | flops 37748736 | bytes 65036288 | tf_op jit(solution)/shard_map/while/body/eval_jaxpr/convert_element_type | solution.py:106
  886.8 16.2 %copy.95 = bf16[2,2048,3,1,192]{4,0,3,2,1:T(2,128)(2,1)} copy(bf16[2,2048,3,1,192]{1,4,3,2,0:T(8,128)(2,1)} %get-tuple-element.77) | data formatting | bytes 9437184 | tf_op jit(solution)/shard_map/while | solution.py:270
  909.1 137.3 %all-to-all-done.4 = bf16[2,2048,3,1,192]{4,0,3,2,1:T(2,128)(2,1)} async-done(((bf16[2,2048,3,1,192]{4,0,3,2,1:T(2,128)(2,1)}), bf16[2,2048,3,1,192]{4,0,3,2,1:T(2,128)(2,1)}, u32[]{:S(2)}, u32[]{:S(2)}) %all-to-all-start.4) | async-done | bytes 4718624 | tf_op jit(solution)/shard_map/all_to_all | solution.py:271
  1046.4 16.9 %copy.102 = bf16[2,4,512,3,1,192]{2,1,5,3,0,4:T(4,128)(2,1)} copy(bf16[2,4,512,3,1,192]{5,0,3,2,1,4:T(2,128)(2,1)} %bitcast.59) | data formatting | bytes 9437184 | tf_op jit(solution)/shard_map/all_to_all | solution.py:271
  1063.3 9.3 copy.97
  1089.8 10.6 fusion.117
  1104.7 44.6 %reduce-scatter.5.cloned.1.call-done = f32[96,2304]{1,0:T(8,128)} async-done(((f32[768,2304]{1,0:T(8,128)}), f32[96,2304]{1,0:T(8,128)}) %reduce-scatter.5.cloned.1.call-update) | async-done | bytes 884752 | tf_op jit(solution)/shard_map/reduce_scatter | solution.py:287
  1159.2 25.1 %all-reduce.16 = (bf16[768]{0:T(1024)(128)(2,1)S(1)}, bf16[768]{0:T(1024)(128)(2,1)S(1)}, bf16[1536]{0:T(1024)(128)(2,1)S(1)}, bf16[768]{0:T(1024)(128)(2,1)S(1)...) all-reduce(f32[768]{0:T(1024)S(1)} %get-tuple-element.143, ...), channel_id=2, replica_groups=mesh['fsdp'=8,'seq'=4] {'fsdp'}, use_global_device_ids=true, to_apply=%region_30.31.clone | all-reduce | flops 9216 | bytes 55296
  1184.9 11.8 all-reduce.18
  1205.3 24.9 %all-reduce.22.cloned.1.call-done = (bf16[96,2304]{1,0:T(8,128)(2,1)}, bf16[96,768]{1,0:T(8,128)(2,1)}, bf16[96,3072]{1,0:T(8,128)(2,1)}, bf16[384,768]{1,0:T(8,128)(2,1)}) async-done(((bf16[96,2304]{1,0:T(8,128)(2,1)}, bf16[96,768]{1,0:T(8,128)(2,1)}, bf16[96,3072]{1,0:T(8,128)(2,1)}, bf16[384,768]{1,0:T(8,128)(2,1)}), (bf16[96,2304]{1,0:T(8,128)(2,1)}, bf16[96,768]{1,0:T(8,128)(2,1)}, ...) | async-done | bytes 1769488 | tf_op jit(solution)/shard_map/psum | solution.py:301
  (461 shorter events, 439.7 us)
Async XLA Ops:
  7.2 42.3 %copy-start.5 = (bf16[2,512,768]{2,1,0:T(8,128)(2,1)S(1)}, bf16[2,512,768]{2,1,0:T(8,128)(2,1)}, u32[]{:S(2)}) copy-start(bf16[2,512,768]{2,1,0:T(8,128)(2,1)} %param.21) | copy-start | bytes 4718596
  7.2 42.9 %all-gather.6.cloned.1.call-start = ((), (), s32[]{:S(2)}) async-start(), calls=%async_computation.9 | async-start | bytes 3981312 | tf_op jit(solution)/shard_map/all_gather | solution.py:151
  7.9 390.7 %all-gather.8.cloned.1.call-start = ((), (), s32[]{:S(2)}) async-start(), calls=%async_computation.10 | async-start | bytes 1327104 | tf_op jit(solution)/shard_map/all_gather | solution.py:153
  8.7 395.6 %all-gather.10.cloned.1.call-start = ((), (), s32[]{:S(2)}) async-start(), calls=%async_computation.11 | async-start | bytes 5308416 | tf_op jit(solution)/shard_map/all_gather | solution.py:157
  87.8 106.9 %all-to-all-start = ((bf16[2,512,3,4,192]{1,0,4,2,3:T(2,128)(2,1)}), bf16[2,512,3,4,192]{1,0,4,2,3:T(2,128)(2,1)}, u32[]{:S(2)}, u32[]{:S(2)}) async-start(bf16[2,512,3,4,192]{1,0,4,2,3:T(2,128)(2,1)} %copy.86), calls=%async_computation | async-start | bytes 9437184 | tf_op jit(solution)/shard_map/all_to_all | solution.py:190
  195.3 20.8 %all-to-all-start.1 = ((bf16[2,512,1,4,1]{1,0,4,2,3:T(2,128)(2,1)}), bf16[2,512,1,4,1]{1,0,4,2,3:T(2,128)(2,1)S(1)}, u32[]{:S(2)}, u32[]{:S(2)}) async-start(bf16[2,512,1,4,1]{1,0,4,2,3:T(2,128)(2,1)} %broadcast_in_dim.114), calls=%async_computation.1 | async-start | bytes 16384 | tf_op jit(solution)/shard_map/all_to_all | solution.py:191
  198.5 216.9 %all-gather.12.cloned.1.call-start = ((), (), s32[]{:S(2)}) async-start(), calls=%async_computation.12 | async-start | bytes 5308416 | tf_op jit(solution)/shard_map/all_gather | solution.py:159
  329.2 11.4 copy-start.60
  335.3 63.3 %copy-start.6 = (bf16[2,512,768]{2,1,0:T(8,128)(2,1)S(1)}, bf16[2,512,768]{2,1,0:T(8,128)(2,1)}, u32[]{:S(2)}) copy-start(bf16[2,512,768]{2,1,0:T(8,128)(2,1)} %param.21) | copy-start | bytes 4718596
  335.3 52.5 %all-to-all-start.2 = ((bf16[2,2048,1,192]{3,0,2,1:T(2,128)(2,1)}), bf16[2,2048,1,192]{3,0,2,1:T(2,128)(2,1)}, u32[]{:S(2)}, u32[]{:S(2)}) async-start(bf16[2,2048,1,192]{3,0,2,1:T(2,128)(2,1)} %bitcast.418), calls=%async_computation.2 | async-start | bytes 4194304 | tf_op jit(solution)/shard_map/all_to_all | solution.py:195
  340.5 747.7 %reduce-scatter.7.cloned.1.call-start = ((), (), s32[]{:S(2)}) async-start(), calls=%async_computation.14 | async-start | bytes 2654208 | tf_op jit(solution)/shard_map/reduce_scatter | solution.py:289
  415.4 13.7 %copy-start.54 = (s32[2,512]{1,0:T(2,128)S(1)}, s32[2,512]{1,0:T(2,128)}, u32[]{:S(2)}) copy-start(s32[2,512]{1,0:T(2,128)} %param.25) | copy-start | bytes 12292
  415.5 13.7 %copy-start.55 = (s32[2,512]{1,0:T(2,128)S(1)}, s32[2,512]{1,0:T(2,128)}, u32[]{:S(2)}) copy-start(s32[2,512]{1,0:T(2,128)} %param.24) | copy-start | bytes 12292
  470.0 22.1 %slice-start.4 = ((s8[4718592]{0:T(1024)(128)(4,1)}), s8[4194304]{0:T(1024)(128)(4,1)S(1)}, s32[]{:S(2)}) async-start(s8[4718592]{0:T(1024)(128)(4,1)} %bitcast.450), calls=%async_computation.22 | async-start | bytes 8388608
  473.6 18.5 %copy-start.35 = (bf16[1024,768]{1,0:T(8,128)(2,1)}, bf16[1024,768]{1,0:T(8,128)(2,1)S(1)}, u32[]{:S(2)}) copy-start(bf16[1024,768]{1,0:T(8,128)(2,1)S(1)} %get-tuple-element.202) | copy-start | bytes 4718596
  473.6 18.5 %slice-start.5 = ((s8[4718592]{0:T(1024)(128)(4,1)}), s8[524288]{0:T(1024)(128)(4,1)S(1)}, s32[]{:S(2)}) async-start(s8[4718592]{0:T(1024)(128)(4,1)} %bitcast.450), calls=%async_computation.23 | async-start | bytes 1048576
  507.7 592.7 %reduce-scatter.9.cloned.1.call-start = ((), (), s32[]{:S(2)}) async-start(), calls=%async_computation.15 | async-start | bytes 10616832 | tf_op jit(solution)/shard_map/reduce_scatter | solution.py:293
  528.6 40.6 %all-to-all-start.3 = ((bf16[2,512,4,192]{1,0,3,2:T(2,128)(2,1)}), bf16[2,512,4,192]{1,0,3,2:T(2,128)(2,1)S(1)}, u32[]{:S(2)}, u32[]{:S(2)}) async-start(bf16[2,512,4,192]{1,0,3,2:T(2,128)(2,1)} %reshape.704), calls=%async_computation.3 | async-start | bytes 3145728 | tf_op jit(solution)/shard_map/all_to_all | solution.py:263
  532.8 569.8 %reduce-scatter.11.cloned.1.call-start = ((), (), s32[]{:S(2)}) async-start(), calls=%async_computation.16 | async-start | bytes 10616832 | tf_op jit(solution)/shard_map/reduce_scatter | solution.py:295
  572.6 27.3 %copy-start.26 = (f32[3,512]{1,0:T(4,128)}, f32[3,512]{1,0:T(4,128)S(1)}, u32[]{:S(2)}) copy-start(f32[3,512]{1,0:T(4,128)S(1)} %get-tuple-element.435) | copy-start | bytes 18436 | tf_op jit(solution)/shard_map/while
  576.0 18.4 %copy-start.10 = (bf16[512,1,1,192]{0,3,2,1:T(8,128)(2,1)}, bf16[512,1,1,192]{0,3,2,1:T(8,128)(2,1)S(1)}, u32[]{:S(2)}) copy-start(bf16[512,1,1,192]{0,3,2,1:T(8,128)(2,1)S(1)} %get-tuple-element.433) | copy-start | bytes 589828 | tf_op jit(solution)/shard_map/while
  580.3 42.4 %copy-start.4 = (pred[512,2048]{1,0:T(8,128)(4,1)}, pred[512,2048]{1,0:T(8,128)(4,1)S(1)}, u32[]{:S(2)}) copy-start(pred[512,2048]{1,0:T(8,128)(4,1)S(1)} %get-tuple-element.448) | copy-start | bytes 3145732 | tf_op jit(solution)/shard_map/while
  696.7 18.2 %copy-start.11 = (bf16[512,1,1,192]{0,3,2,1:T(8,128)(2,1)S(1)}, bf16[512,1,1,192]{0,3,2,1:T(8,128)(2,1)}, u32[]{:S(2)}) copy-start(bf16[512,1,1,192]{0,3,2,1:T(8,128)(2,1)} %copy-done.10) | copy-start | bytes 589828 | tf_op jit(solution)/shard_map/while
  729.0 27.3 %copy-start.26 = (f32[3,512]{1,0:T(4,128)}, f32[3,512]{1,0:T(4,128)S(1)}, u32[]{:S(2)}) copy-start(f32[3,512]{1,0:T(4,128)S(1)} %get-tuple-element.435) | copy-start | bytes 18436 | tf_op jit(solution)/shard_map/while
  732.4 18.5 %copy-start.10 = (bf16[512,1,1,192]{0,3,2,1:T(8,128)(2,1)}, bf16[512,1,1,192]{0,3,2,1:T(8,128)(2,1)S(1)}, u32[]{:S(2)}) copy-start(bf16[512,1,1,192]{0,3,2,1:T(8,128)(2,1)S(1)} %get-tuple-element.433) | copy-start | bytes 589828 | tf_op jit(solution)/shard_map/while
  736.8 41.9 %copy-start.4 = (pred[512,2048]{1,0:T(8,128)(4,1)}, pred[512,2048]{1,0:T(8,128)(4,1)S(1)}, u32[]{:S(2)}) copy-start(pred[512,2048]{1,0:T(8,128)(4,1)S(1)} %get-tuple-element.448) | copy-start | bytes 3145732 | tf_op jit(solution)/shard_map/while
  847.8 18.1 %copy-start.11 = (bf16[512,1,1,192]{0,3,2,1:T(8,128)(2,1)S(1)}, bf16[512,1,1,192]{0,3,2,1:T(8,128)(2,1)}, u32[]{:S(2)}) copy-start(bf16[512,1,1,192]{0,3,2,1:T(8,128)(2,1)} %copy-done.10) | copy-start | bytes 589828 | tf_op jit(solution)/shard_map/while
  903.0 143.4 %all-to-all-start.4 = ((bf16[2,2048,3,1,192]{4,0,3,2,1:T(2,128)(2,1)}), bf16[2,2048,3,1,192]{4,0,3,2,1:T(2,128)(2,1)}, u32[]{:S(2)}, u32[]{:S(2)}) async-start(bf16[2,2048,3,1,192]{4,0,3,2,1:T(2,128)(2,1)} %copy.95), calls=%async_computation.4 | async-start | bytes 12582912 | tf_op jit(solution)/shard_map/all_to_all | solution.py:271
  908.3 241.0 %reduce-scatter.5.cloned.1.call-start = ((), (), s32[]{:S(2)}) async-start(), calls=%async_computation.13 | async-start | bytes 7962624 | tf_op jit(solution)/shard_map/reduce_scatter | solution.py:287
  1084.7 145.5 %all-reduce.22.cloned.1.call-start = ((), (), s32[]{:S(2)}) async-start(), calls=%async_computation.17 | async-start | bytes 3538944 | tf_op jit(solution)/shard_map/psum | solution.py:301
  1104.7 51.4 %copy-start.50 = (f32[1,4,2,128]{3,1,2,0:T(4,128)S(1)}, f32[1,4,2,128]{3,1,2,0:T(4,128)}, u32[]{:S(2)}) copy-start(f32[1,4,2,128]{3,1,2,0:T(4,128)} %copy-done.49) | copy-start | bytes 12292
  1104.7 51.4 %copy-start.44 = (f32[1024]{0:T(1024)S(1)}, f32[1024]{0:T(1024)}, u32[]{:S(2)}) copy-start(f32[1024]{0:T(1024)} %copy-done.43) | copy-start | bytes 12292
  (84 other events, 350.4 us)
Sparse Core Ops, SparseCore 0:
  9.9 36.8 all-gather.5
  48.7 24.0 all-gather.7
  74.7 38.9 all-gather.9
  201.0 40.8 all-gather.11
  507.8 43.0 reduce-scatter.6
  554.7 76.4 reduce-scatter.8
  635.2 76.4 reduce-scatter.10
  1084.8 64.5 reduce-scatter.4
  1153.2 76.9 all-reduce.21
where the time goes:
time: 1260 us; the launch traced here: 1250 us
  waiting for transfers between devices  373 us (30%)
  matrix products  356 us (28%)
  other arithmetic  177 us (14%)
  local copies, waits for them, and re-layouts  159 us (13%)
  blocking collectives  112 us (9%)
  loops' own time  24.8 us (2%)
  starting transfers between devices  23.5 us (2%)
  between operations  21.1 us (2%)
    all_to_all x1, waiting for transfers between devices, local(): lax.all_to_all(grad_joint_heads, 'seq', split_axis=1, concat_axis=3, tile...  137 us
    all_to_all x1, waiting for transfers between devices, local(): lax.all_to_all(joint_low, 'seq', split_axis=3, concat_axis=1, tiled=True)  102 us
    convert_element_type x4, other arithmetic, back_sequence(): grad_scores = (probs * (grad_probs - center)).astype(jnp.bfloat16)  85.3 us
    dot_general x8, matrix products, back_sequence(): jnp.einsum('qhd,khd->hqk', grad_block, values, preferred_element_type=jnp...  73.9 us
    dot_general x16, matrix products, block_scores(): jnp.einsum('qhd,khd->hqk', query_block, keys, preferred_element_type=jnp....  54.2 us
    unnamed x2, blocking collectives  51.7 us
    dot_general x8, matrix products, back_sequence(): jnp.einsum('hqk,qhd->khd', probs_low, grad_block, preferred_element_type=...  46.4 us
    reduce_scatter x1, waiting for transfers between devices, local(): lax.psum_scatter(grad_jointweight, 'fsdp', scatter_dimension=0, tiled=True)  44.6 us
  transfers between devices with their start and end apart: 14, of which 6 were waited for; matrix products, arithmetic and copies ran while one was open for 48% of the time, Pallas kernels for 0%

commit v1 on v0

--- a/solution.py
+++ b/solution.py
@@ -213,7 +213,7 @@
     layer_out = result.astype(jnp.bfloat16).reshape(tokens.shape)
     error = result - teacher.astype(jnp.float32).reshape(rows, width)
     local_sum = jnp.sum(weight * jnp.sum(error * error, -1))
-    total_sum, total_count = lax.psum((local_sum, local_count), ("fsdp", "seq"))
+    total_sum, total_count = lax.psum(lax.psum((local_sum, local_count), "seq"), "fsdp")
     distill_loss = total_sum / (width * total_count)
     token_total = rows * lax.axis_size("fsdp") * groups
     factor = token_total / total_count

time: 1260 us -> 1240 us (0.984)
  blocking collectives: 112 us -> 96.2 us
    unnamed x2 -> x1, blocking collectives: 51.7 us -> 26.6 us
    psum x1 -> x3, blocking collectives: 39.5 us -> 48.9 us  [the longest x2 38.5 us: local(): lax.psum(lax.psum((local_sum, local_count), 'seq'), 'fsdp')]
  transfers between devices with their start and end apart: 14 -> 14, of which waited for: 6 -> 6; matrix products, arithmetic and copies ran while one was open for 48% -> 49% of each run, Pallas kernels for 0% -> 0%
where the time goes in v1:
time: 1240 us; the launch traced here: 1230 us
  waiting for transfers between devices  372 us (30%)
  matrix products  355 us (29%)
  other arithmetic  179 us (14%)
  local copies, waits for them, and re-layouts  159 us (13%)
  blocking collectives  96.2 us (8%)
  loops' own time  24.8 us (2%)
  starting transfers between devices  22.9 us (2%)
  between operations  21.2 us (2%)
    all_to_all x1, waiting for transfers between devices, local(): lax.all_to_all(grad_joint_heads, 'seq', split_axis=1, concat_axis=3, tile...  137 us
    all_to_all x1, waiting for transfers between devices, local(): lax.all_to_all(joint_low, 'seq', split_axis=3, concat_axis=1, tiled=True)  102 us
    convert_element_type x4, other arithmetic, back_sequence(): grad_scores = (probs * (grad_probs - center)).astype(jnp.bfloat16)  86.1 us
    dot_general x8, matrix products, back_sequence(): jnp.einsum('qhd,khd->hqk', grad_block, values, preferred_element_type=jnp...  73.7 us
    dot_general x16, matrix products, block_scores(): jnp.einsum('qhd,khd->hqk', query_block, keys, preferred_element_type=jnp....  54.3 us
    dot_general x8, matrix products, back_sequence(): jnp.einsum('hqk,qhd->khd', probs_low, grad_block, preferred_element_type=...  46 us
    reduce_scatter x1, waiting for transfers between devices, local(): lax.psum_scatter(grad_jointweight, 'fsdp', scatter_dimension=0, tiled=True)  43.2 us
    psum x2, blocking collectives, local(): lax.psum(lax.psum((local_sum, local_count), 'seq'), 'fsdp')  38.5 us
  transfers between devices with their start and end apart: 14, of which 6 were waited for; matrix products, arithmetic and copies ran while one was open for 49% of the time, Pallas kernels for 0%

profile of v1, /device:TPU:0, one launch (start us, length us, event | category | flops | bytes accessed | tf_op | source)
XLA Modules:
  0.0 1229.8 jit_solution(10245570874759908243)
XLA Ops:
  19.6 26.6 %all-reduce.17 = (bf16[768]{0:T(1024)(128)(2,1)S(1)}, bf16[768]{0:T(1024)(128)(2,1)S(1)}, bf16[1536]{0:T(1024)(128)(2,1)S(1)}, bf16[768]{0:T(1024)(128)(2,1)}, b...) all-reduce(bf16[768]{0:T(1024)(128)(2,1)S(1)} %dynamic-update-slice, ...), channel_id=1, replica_groups=mesh['fsdp'=8,'seq'=4] {'fsdp'}, use_global_device_ids=true, to_apply=%add.1 | all-reduce | flops 6144 | bytes 24576
  57.6 12.8 %reshape.747 = bf16[2,512,3,4,192]{4,3,2,1,0:T(4,128)(2,1)} reshape(bf16[1024,2304]{1,0:T(8,128)(2,1)} %add_convert_fusion) | data formatting | bytes 9437184 | tf_op jit(solution)/shard_map/reshape | solution.py:181
  70.5 17.3 %copy.86 = bf16[2,512,3,4,192]{1,0,4,2,3:T(2,128)(2,1)} copy(bf16[2,512,3,4,192]{4,3,2,1,0:T(4,128)(2,1)} %reshape.747) | data formatting | bytes 9437184 | tf_op jit(solution)/shard_map/reshape | solution.py:181
  92.9 101.8 %all-to-all-done = bf16[2,512,3,4,192]{1,0,4,2,3:T(2,128)(2,1)} async-done(((bf16[2,512,3,4,192]{1,0,4,2,3:T(2,128)(2,1)}), bf16[2,512,3,4,192]{1,0,4,2,3:T(2,128)(2,1)}, u32[]{:S(2)}, u32[]{:S(2)}) %all-to-all-start) | async-done | bytes 4718624 | tf_op jit(solution)/shard_map/all_to_all | solution.py:190
  216.1 113.0 %while.22 = (s32[]{:T(128)}, bf16[2,2048,192]{1,2,0:T(8,128)(2,1)}, f32[2,3,2048]{2,1,0:T(4,128)S(1)}, bf16[2,2048,3,1,192]{1,4,2,3,0:T(8,128)(2,1)}, bf16[2,204...) while((s32[]{:T(128)}, bf16[2,2048,192]{1,2,0:T(8,128)(2,1)}, ...), condition=%wide.region_11.12_spmd, body=%wide.region_2.11_spmd.sunk | while | flops 3393599488 | bytes 199532768 | solution.py:79
  349.4 38.3 %all-to-all-done.2 = bf16[2,2048,1,192]{3,0,2,1:T(2,128)(2,1)} async-done(((bf16[2,2048,1,192]{3,0,2,1:T(2,128)(2,1)}), bf16[2,2048,1,192]{3,0,2,1:T(2,128)(2,1)}, u32[]{:S(2)}, u32[]{:S(2)}) %all-to-all-start.2) | async-done | bytes 1572896 | tf_op jit(solution)/shard_map/all_to_all | solution.py:195
  404.2 11.2 fusion.113
  415.4 13.7 %multiply_reduce_fusion.6 = (f32[1024]{0:T(1024)S(1)}, f32[1024,768]{1,0:T(8,128)}) fusion(bf16[2,512,768]{2,1,0:T(8,128)(2,1)} %param.22, f32[768]{0:T(1024)S(1)} %convert_element_type.248, f32[1024,768]{1,0:T(8,128)S(1)} %copy-done.15, bf16[3072,768]{1,0:T(8,128)(2,1)} %all-gather.12.cloned.1.call-done, f32[1024,3072]{1,0:T(8,128)} %fusion.113, ...), kind=kOutput, calls=%fused_computation.184 | convolution fusion | flops 4868013056 | bytes 25185280 | tf_op jit(solution)/shard_map/dot_general | solution.py:211
  429.7 10.4 all-reduce.16
  440.2 13.2 %psum.115 = f32[]{:T(128)} all-reduce(f32[]{:T(128)} %get-tuple-element.182), channel_id=1, replica_groups=mesh['fsdp'=8,'seq'=4] {'fsdp'}, use_global_device_ids=true, to_apply=%region_20.21 | all-reduce | flops 1 | bytes 8 | tf_op jit(solution)/shard_map/psum | solution.py:216
  459.9 18.4 %convert_reduce_fusion = (f32[3072]{0:T(1024)}, bf16[1024,3072]{1,0:T(8,128)(2,1)S(1)}) fusion(f32[1024,3072]{1,0:T(8,128)} %fusion.113, f32[3072]{0:T(1024)S(1)} %bitcast.448, bf16[1024,768]{1,0:T(8,128)(2,1)S(1)} %get-tuple-element.203, bf16[3072,768]{1,0:T(8,128)(2,1)} %all-gather.12.cloned.1.call-done), kind=kOutput, calls=%fused_computation.151 | convolution fusion | flops 4916769792 | bytes 25190400 | tf_op jit(solution)/shard_map/rd,fd->rf/dot_general | solution.py:244
  492.8 11.0 fusion.112
  517.4 13.0 %fusion.114 = f32[3072,768]{1,0:T(8,128)} fusion(bf16[1024,768]{1,0:T(8,128)(2,1)S(1)} %copy-done.36, f32[1024,3072]{1,0:T(8,128)} %fusion.113, f32[3072]{0:T(1024)S(1)} %bitcast.449), kind=kOutput, calls=%fused_computation.222 | convolution fusion | flops 4863295488 | bytes 23605248 | tf_op jit(solution)/shard_map/rf,rd->fd/dot_general | solution.py:241
  530.4 24.6 %all-to-all-done.3 = bf16[2,512,4,192]{1,0,3,2:T(2,128)(2,1)S(1)} async-done(((bf16[2,512,4,192]{1,0,3,2:T(2,128)(2,1)}), bf16[2,512,4,192]{1,0,3,2:T(2,128)(2,1)S(1)}, u32[]{:S(2)}, u32[]{:S(2)}) %all-to-all-start.3) | async-done | bytes 1572896 | tf_op jit(solution)/shard_map/all_to_all | solution.py:263
  557.4 314.9 %while.23 = (s32[]{:T(128)}, bf16[2,2048,3,1,192]{1,4,3,2,0:T(8,128)(2,1)}, bf16[2,2048,3,1,192]{1,4,2,3,0:T(8,128)(2,1)}, bf16[2,2048]{1,0:T(2,128)(2,1)S(1)}, ...) while((s32[]{:T(128)}, ...), condition=%wide.region_28.29_spmd, body=%wide.region_23.28_spmd.sunk | while | flops 8274178048 | bytes 657154752 | solution.py:270
  608.6 10.3 multiply_reduce_fusion.14
  618.9 26.9 %multiply_convert_fusion.8 = (bf16[3,512,2048]{2,1,0:T(8,128)(2,1)}, bf16[3,512,2048]{2,1,0:T(8,128)(2,1)}) fusion(f32[3,512,2048]{2,1,0:T(8,128)} %get-tuple-element.455, f32[3,512,2048]{2,1,0:T(8,128)} %copy-done, f32[3,512]{1,0:T(4,128)S(1)} %get-tuple-element.456, f32[3,512]{1,0:T(4,128)S(1)} %get-tuple-element.444, ...), kind=kLoop, calls=%fused_computation.68.clone.1 | loop fusion | flops 37748736 | bytes 65036288 | tf_op jit(solution)/shard_map/while/body/eval_jaxpr/convert_element_type | solution.py:106
  671.5 10.7 multiply_reduce_fusion.15
  682.2 18.3 %multiply_convert_fusion.9 = (bf16[3,512,2048]{2,1,0:T(8,128)(2,1)}, bf16[3,512,2048]{2,1,0:T(8,128)(2,1)}) fusion(f32[3,512,2048]{2,1,0:T(8,128)} %get-tuple-element.461, f32[3,512,2048]{2,1,0:T(8,128)} %fusion.362, f32[3,512]{1,0:T(4,128)} %get-tuple-element.462, f32[3,512]{1,0:T(4,128)S(1)} %get-tuple-element.452, ...), kind=kLoop, calls=%fused_computation.62.clone.1 | loop fusion | flops 37748736 | bytes 65036288 | tf_op jit(solution)/shard_map/while/body/eval_jaxpr/convert_element_type | solution.py:106
  764.2 10.4 multiply_reduce_fusion.14
  774.6 22.8 %multiply_convert_fusion.8 = (bf16[3,512,2048]{2,1,0:T(8,128)(2,1)}, bf16[3,512,2048]{2,1,0:T(8,128)(2,1)}) fusion(f32[3,512,2048]{2,1,0:T(8,128)} %get-tuple-element.455, f32[3,512,2048]{2,1,0:T(8,128)} %copy-done, f32[3,512]{1,0:T(4,128)S(1)} %get-tuple-element.456, f32[3,512]{1,0:T(4,128)S(1)} %get-tuple-element.444, ...), kind=kLoop, calls=%fused_computation.68.clone.1 | loop fusion | flops 37748736 | bytes 65036288 | tf_op jit(solution)/shard_map/while/body/eval_jaxpr/convert_element_type | solution.py:106
  822.7 10.7 multiply_reduce_fusion.15
  833.4 18.0 %multiply_convert_fusion.9 = (bf16[3,512,2048]{2,1,0:T(8,128)(2,1)}, bf16[3,512,2048]{2,1,0:T(8,128)(2,1)}) fusion(f32[3,512,2048]{2,1,0:T(8,128)} %get-tuple-element.461, f32[3,512,2048]{2,1,0:T(8,128)} %fusion.362, f32[3,512]{1,0:T(4,128)} %get-tuple-element.462, f32[3,512]{1,0:T(4,128)S(1)} %get-tuple-element.452, ...), kind=kLoop, calls=%fused_computation.62.clone.1 | loop fusion | flops 37748736 | bytes 65036288 | tf_op jit(solution)/shard_map/while/body/eval_jaxpr/convert_element_type | solution.py:106
  872.3 16.1 %copy.95 = bf16[2,2048,3,1,192]{4,0,3,2,1:T(2,128)(2,1)} copy(bf16[2,2048,3,1,192]{1,4,3,2,0:T(8,128)(2,1)} %get-tuple-element.77) | data formatting | bytes 9437184 | tf_op jit(solution)/shard_map/while | solution.py:270
  894.6 137.4 %all-to-all-done.4 = bf16[2,2048,3,1,192]{4,0,3,2,1:T(2,128)(2,1)} async-done(((bf16[2,2048,3,1,192]{4,0,3,2,1:T(2,128)(2,1)}), bf16[2,2048,3,1,192]{4,0,3,2,1:T(2,128)(2,1)}, u32[]{:S(2)}, u32[]{:S(2)}) %all-to-all-start.4) | async-done | bytes 4718624 | tf_op jit(solution)/shard_map/all_to_all | solution.py:271
  1032.0 17.0 %copy.102 = bf16[2,4,512,3,1,192]{2,1,5,3,0,4:T(4,128)(2,1)} copy(bf16[2,4,512,3,1,192]{5,0,3,2,1,4:T(2,128)(2,1)} %bitcast.59) | data formatting | bytes 9437184 | tf_op jit(solution)/shard_map/all_to_all | solution.py:271
  1049.0 9.3 copy.97
  1074.9 10.8 fusion.117
  1090.0 43.2 %reduce-scatter.5.cloned.1.call-done = f32[96,2304]{1,0:T(8,128)} async-done(((f32[768,2304]{1,0:T(8,128)}), f32[96,2304]{1,0:T(8,128)}) %reduce-scatter.5.cloned.1.call-update) | async-done | bytes 884752 | tf_op jit(solution)/shard_map/reduce_scatter | solution.py:287
  1143.0 25.2 %all-reduce.15 = (f32[]{:T(128)}, bf16[768]{0:T(1024)(128)(2,1)S(1)}, bf16[768]{0:T(1024)(128)(2,1)S(1)}, bf16[1536]{0:T(1024)(128)(2,1)S(1)}, bf16[768]{0:T(102...) all-reduce(f32[]{:T(128)} %get-tuple-element.181, ...), channel_id=1, replica_groups=mesh['fsdp'=8,'seq'=4] {'fsdp'}, use_global_device_ids=true, to_apply=%region_17.18 | all-reduce | flops 9217 | bytes 55304 | tf_op jit(solution)/shard_map/psum | solution.py:216
  1168.8 11.8 all-reduce.18
  1189.9 24.1 %all-reduce.22.cloned.1.call-done = (bf16[96,2304]{1,0:T(8,128)(2,1)}, bf16[96,768]{1,0:T(8,128)(2,1)}, bf16[96,3072]{1,0:T(8,128)(2,1)}, bf16[384,768]{1,0:T(8,128)(2,1)}) async-done(((bf16[96,2304]{1,0:T(8,128)(2,1)}, bf16[96,768]{1,0:T(8,128)(2,1)}, bf16[96,3072]{1,0:T(8,128)(2,1)}, bf16[384,768]{1,0:T(8,128)(2,1)}), (bf16[96,2304]{1,0:T(8,128)(2,1)}, bf16[96,768]{1,0:T(8,128)(2,1)}, ...) | async-done | bytes 1769488 | tf_op jit(solution)/shard_map/psum | solution.py:301
  (462 shorter events, 448.1 us)
Async XLA Ops:
  7.2 42.3 %copy-start.5 = (bf16[2,512,768]{2,1,0:T(8,128)(2,1)S(1)}, bf16[2,512,768]{2,1,0:T(8,128)(2,1)}, u32[]{:S(2)}) copy-start(bf16[2,512,768]{2,1,0:T(8,128)(2,1)} %param.21) | copy-start | bytes 4718596
  7.2 42.9 %all-gather.6.cloned.1.call-start = ((), (), s32[]{:S(2)}) async-start(), calls=%async_computation.9 | async-start | bytes 3981312 | tf_op jit(solution)/shard_map/all_gather | solution.py:151
  7.9 390.6 %all-gather.8.cloned.1.call-start = ((), (), s32[]{:S(2)}) async-start(), calls=%async_computation.10 | async-start | bytes 1327104 | tf_op jit(solution)/shard_map/all_gather | solution.py:153
  8.7 395.5 %all-gather.10.cloned.1.call-start = ((), (), s32[]{:S(2)}) async-start(), calls=%async_computation.11 | async-start | bytes 5308416 | tf_op jit(solution)/shard_map/all_gather | solution.py:157
  87.8 106.9 %all-to-all-start = ((bf16[2,512,3,4,192]{1,0,4,2,3:T(2,128)(2,1)}), bf16[2,512,3,4,192]{1,0,4,2,3:T(2,128)(2,1)}, u32[]{:S(2)}, u32[]{:S(2)}) async-start(bf16[2,512,3,4,192]{1,0,4,2,3:T(2,128)(2,1)} %copy.86), calls=%async_computation | async-start | bytes 9437184 | tf_op jit(solution)/shard_map/all_to_all | solution.py:190
  195.3 20.8 %all-to-all-start.1 = ((bf16[2,512,1,4,1]{1,0,4,2,3:T(2,128)(2,1)}), bf16[2,512,1,4,1]{1,0,4,2,3:T(2,128)(2,1)S(1)}, u32[]{:S(2)}, u32[]{:S(2)}) async-start(bf16[2,512,1,4,1]{1,0,4,2,3:T(2,128)(2,1)} %broadcast_in_dim.114), calls=%async_computation.1 | async-start | bytes 16384 | tf_op jit(solution)/shard_map/all_to_all | solution.py:191
  198.5 216.8 %all-gather.12.cloned.1.call-start = ((), (), s32[]{:S(2)}) async-start(), calls=%async_computation.12 | async-start | bytes 5308416 | tf_op jit(solution)/shard_map/all_gather | solution.py:159
  329.2 11.3 copy-start.60
  335.3 63.3 %copy-start.6 = (bf16[2,512,768]{2,1,0:T(8,128)(2,1)S(1)}, bf16[2,512,768]{2,1,0:T(8,128)(2,1)}, u32[]{:S(2)}) copy-start(bf16[2,512,768]{2,1,0:T(8,128)(2,1)} %param.21) | copy-start | bytes 4718596
  335.3 52.5 %all-to-all-start.2 = ((bf16[2,2048,1,192]{3,0,2,1:T(2,128)(2,1)}), bf16[2,2048,1,192]{3,0,2,1:T(2,128)(2,1)}, u32[]{:S(2)}, u32[]{:S(2)}) async-start(bf16[2,2048,1,192]{3,0,2,1:T(2,128)(2,1)} %bitcast.418), calls=%async_computation.2 | async-start | bytes 4194304 | tf_op jit(solution)/shard_map/all_to_all | solution.py:195
  340.4 732.8 %reduce-scatter.7.cloned.1.call-start = ((), (), s32[]{:S(2)}) async-start(), calls=%async_computation.14 | async-start | bytes 2654208 | tf_op jit(solution)/shard_map/reduce_scatter | solution.py:289
  415.4 13.7 %copy-start.54 = (s32[2,512]{1,0:T(2,128)S(1)}, s32[2,512]{1,0:T(2,128)}, u32[]{:S(2)}) copy-start(s32[2,512]{1,0:T(2,128)} %param.25) | copy-start | bytes 12292
  415.4 13.7 %copy-start.55 = (s32[2,512]{1,0:T(2,128)S(1)}, s32[2,512]{1,0:T(2,128)}, u32[]{:S(2)}) copy-start(s32[2,512]{1,0:T(2,128)} %param.24) | copy-start | bytes 12292
  454.1 24.2 %slice-start.4 = ((s8[4718592]{0:T(1024)(128)(4,1)}), s8[4194304]{0:T(1024)(128)(4,1)S(1)}, s32[]{:S(2)}) async-start(s8[4718592]{0:T(1024)(128)(4,1)} %bitcast.450), calls=%async_computation.22 | async-start | bytes 8388608
  459.9 18.5 %copy-start.35 = (bf16[1024,768]{1,0:T(8,128)(2,1)}, bf16[1024,768]{1,0:T(8,128)(2,1)S(1)}, u32[]{:S(2)}) copy-start(bf16[1024,768]{1,0:T(8,128)(2,1)S(1)} %get-tuple-element.203) | copy-start | bytes 4718596
  459.9 18.5 %slice-start.5 = ((s8[4718592]{0:T(1024)(128)(4,1)}), s8[524288]{0:T(1024)(128)(4,1)S(1)}, s32[]{:S(2)}) async-start(s8[4718592]{0:T(1024)(128)(4,1)} %bitcast.450), calls=%async_computation.23 | async-start | bytes 1048576
  492.7 593.0 %reduce-scatter.9.cloned.1.call-start = ((), (), s32[]{:S(2)}) async-start(), calls=%async_computation.15 | async-start | bytes 10616832 | tf_op jit(solution)/shard_map/reduce_scatter | solution.py:293
  513.7 41.3 %all-to-all-start.3 = ((bf16[2,512,4,192]{1,0,3,2:T(2,128)(2,1)}), bf16[2,512,4,192]{1,0,3,2:T(2,128)(2,1)S(1)}, u32[]{:S(2)}, u32[]{:S(2)}) async-start(bf16[2,512,4,192]{1,0,3,2:T(2,128)(2,1)} %reshape.704), calls=%async_computation.3 | async-start | bytes 3145728 | tf_op jit(solution)/shard_map/all_to_all | solution.py:263
  517.3 570.6 %reduce-scatter.11.cloned.1.call-start = ((), (), s32[]{:S(2)}) async-start(), calls=%async_computation.16 | async-start | bytes 10616832 | tf_op jit(solution)/shard_map/reduce_scatter | solution.py:295
  558.5 27.5 %copy-start.26 = (f32[3,512]{1,0:T(4,128)}, f32[3,512]{1,0:T(4,128)S(1)}, u32[]{:S(2)}) copy-start(f32[3,512]{1,0:T(4,128)S(1)} %get-tuple-element.436) | copy-start | bytes 18436 | tf_op jit(solution)/shard_map/while
  561.8 18.6 %copy-start.10 = (bf16[512,1,1,192]{0,3,2,1:T(8,128)(2,1)}, bf16[512,1,1,192]{0,3,2,1:T(8,128)(2,1)S(1)}, u32[]{:S(2)}) copy-start(bf16[512,1,1,192]{0,3,2,1:T(8,128)(2,1)S(1)} %get-tuple-element.434) | copy-start | bytes 589828 | tf_op jit(solution)/shard_map/while
  566.2 42.4 %copy-start.4 = (pred[512,2048]{1,0:T(8,128)(4,1)}, pred[512,2048]{1,0:T(8,128)(4,1)S(1)}, u32[]{:S(2)}) copy-start(pred[512,2048]{1,0:T(8,128)(4,1)S(1)} %get-tuple-element.449) | copy-start | bytes 3145732 | tf_op jit(solution)/shard_map/while
  682.2 18.3 %copy-start.11 = (bf16[512,1,1,192]{0,3,2,1:T(8,128)(2,1)S(1)}, bf16[512,1,1,192]{0,3,2,1:T(8,128)(2,1)}, u32[]{:S(2)}) copy-start(bf16[512,1,1,192]{0,3,2,1:T(8,128)(2,1)} %copy-done.10) | copy-start | bytes 589828 | tf_op jit(solution)/shard_map/while
  714.7 27.3 %copy-start.26 = (f32[3,512]{1,0:T(4,128)}, f32[3,512]{1,0:T(4,128)S(1)}, u32[]{:S(2)}) copy-start(f32[3,512]{1,0:T(4,128)S(1)} %get-tuple-element.436) | copy-start | bytes 18436 | tf_op jit(solution)/shard_map/while
  718.0 18.5 %copy-start.10 = (bf16[512,1,1,192]{0,3,2,1:T(8,128)(2,1)}, bf16[512,1,1,192]{0,3,2,1:T(8,128)(2,1)S(1)}, u32[]{:S(2)}) copy-start(bf16[512,1,1,192]{0,3,2,1:T(8,128)(2,1)S(1)} %get-tuple-element.434) | copy-start | bytes 589828 | tf_op jit(solution)/shard_map/while
  722.4 41.9 %copy-start.4 = (pred[512,2048]{1,0:T(8,128)(4,1)}, pred[512,2048]{1,0:T(8,128)(4,1)S(1)}, u32[]{:S(2)}) copy-start(pred[512,2048]{1,0:T(8,128)(4,1)S(1)} %get-tuple-element.449) | copy-start | bytes 3145732 | tf_op jit(solution)/shard_map/while
  833.4 18.0 %copy-start.11 = (bf16[512,1,1,192]{0,3,2,1:T(8,128)(2,1)S(1)}, bf16[512,1,1,192]{0,3,2,1:T(8,128)(2,1)}, u32[]{:S(2)}) copy-start(bf16[512,1,1,192]{0,3,2,1:T(8,128)(2,1)} %copy-done.10) | copy-start | bytes 589828 | tf_op jit(solution)/shard_map/while
  888.5 143.5 %all-to-all-start.4 = ((bf16[2,2048,3,1,192]{4,0,3,2,1:T(2,128)(2,1)}), bf16[2,2048,3,1,192]{4,0,3,2,1:T(2,128)(2,1)}, u32[]{:S(2)}, u32[]{:S(2)}) async-start(bf16[2,2048,3,1,192]{4,0,3,2,1:T(2,128)(2,1)} %copy.95), calls=%async_computation.4 | async-start | bytes 12582912 | tf_op jit(solution)/shard_map/all_to_all | solution.py:271
  893.9 239.4 %reduce-scatter.5.cloned.1.call-start = ((), (), s32[]{:S(2)}) async-start(), calls=%async_computation.13 | async-start | bytes 7962624 | tf_op jit(solution)/shard_map/reduce_scatter | solution.py:287
  1070.3 143.7 %all-reduce.22.cloned.1.call-start = ((), (), s32[]{:S(2)}) async-start(), calls=%async_computation.17 | async-start | bytes 3538944 | tf_op jit(solution)/shard_map/psum | solution.py:301
  1090.0 49.9 %copy-start.50 = (f32[1,4,2,128]{3,1,2,0:T(4,128)S(1)}, f32[1,4,2,128]{3,1,2,0:T(4,128)}, u32[]{:S(2)}) copy-start(f32[1,4,2,128]{3,1,2,0:T(4,128)} %copy-done.49) | copy-start | bytes 12292
  1090.0 50.0 %copy-start.44 = (f32[1024]{0:T(1024)S(1)}, f32[1024]{0:T(1024)}, u32[]{:S(2)}) copy-start(f32[1024]{0:T(1024)} %copy-done.43) | copy-start | bytes 12292
  (84 other events, 346.0 us)
Sparse Core Ops, SparseCore 0:
  9.9 36.8 all-gather.5
  48.7 24.0 all-gather.7
  74.7 38.9 all-gather.9
  200.9 40.8 all-gather.11
  492.8 39.7 reduce-scatter.6
  536.4 76.4 reduce-scatter.8
  616.8 76.4 reduce-scatter.10
  1070.5 62.7 reduce-scatter.4
  1137.0 76.9 all-reduce.21
